TPU v7x, 32 devices: a whole 2x2x4 slice. The times are simulated.
32 devices in a mesh: dp: 2 (over core), ctx: 4 (over z), fsdp: 4 (over y, x).
Axes of the slice: x: 2, y: 2, z: 4, core: 2. Of those that a mesh axis runs over, the one named last changes fastest.
Arguments:
- tokens: bfloat16 [8, 2, 1024, 2048], P(('dp', 'fsdp'), None, 'ctx'), may hold values from -6 to 6
- cotangent: bfloat16 [8, 2, 1024, 2048], P(('dp', 'fsdp'), None, 'ctx'), may hold values from -6 to 6
- lengths: int32 [8, 2], P(('dp', 'fsdp')), may hold values from 513 to 1024, as said below
- deal: int32 [8, 2, 8], P(('dp', 'fsdp')), may hold values from 0 to 7, each once within a row
- ln_gain: bfloat16 [2048], P('fsdp'), may hold values from 0.5 to 1.5
- ln_bias: bfloat16 [2048], P('fsdp'), may hold values from -1 to 1
- w_qkv: bfloat16 [2048, 6144], P('fsdp'), may hold values from -0.125 to 0.125
- b_qkv: bfloat16 [6144], P('fsdp'), may hold values from -1 to 1
- w_out: bfloat16 [2048, 2048], P('fsdp'), may hold values from -3 to 3
- b_out: bfloat16 [2048], P('fsdp'), may hold values from -2.5 to 2.5
- w_up: bfloat16 [2048, 8192], P('fsdp'), may hold values from -0.125 to 0.125
- b_up: bfloat16 [8192], P('fsdp'), may hold values from -1 to 1
- w_down: bfloat16 [8192, 2048], P('fsdp'), may hold values from -0.0625 to 0.0625
- b_down: bfloat16 [2048], P('fsdp'), may hold values from -2.5 to 2.5
Outputs:
- outputs: bfloat16 [8, 2, 1024, 2048], P(('dp', 'fsdp'), None, 'ctx')
- input_grad: bfloat16 [8, 2, 1024, 2048], P(('dp', 'fsdp'), None, 'ctx')
- grad_ln_gain: float32 [2048], P('fsdp')
- grad_ln_bias: float32 [2048], P('fsdp')
- grad_w_qkv: float32 [2048, 6144], P('fsdp')
- grad_b_qkv: float32 [6144], P('fsdp')
- grad_w_out: float32 [2048, 2048], P('fsdp')
- grad_b_out: float32 [2048], P('fsdp')
- grad_w_up: float32 [2048, 8192], P('fsdp')
- grad_b_up: float32 [8192], P('fsdp')
- grad_w_down: float32 [8192, 2048], P('fsdp')
- grad_b_down: float32 [2048], P('fsdp')
Inputs may be any that keep to these rules, and one draw needn't show every extreme that they name: lengths[g, m] tokens fill the first positions of a sequence, the rest is padding; in every draw one sequence is exactly 1024 long and one exactly 513. Each row of deal is a permutation of the 8 blocks of a sequence.
All inputs are finite; a program needn't handle non-finite values.
Results may differ from a plain program's by a relative error of at most 0.02.
Values may be sent and summed in bfloat16 or wider, within the bound.
No kernel may reach another device: no remote copies, remote signals or barrier semaphores. Data moves between devices by JAX's collectives and lax.ppermute only.
A program may use at most 832 MiB of HBM per device.

v0:
```python
import jax
import jax.numpy as jnp
from jax import lax
from jax.sharding import PartitionSpec as P

HEAD_DIM = 64
ROT = 32
EPS = 1e-05
BASE = 10000.0


def contract_rows(left, right):
    return lax.dot_general(
        left, right, (((0,), (0,)), ((), ())), preferred_element_type=jnp.float32
    )


def contract_cols(left, right):
    return lax.dot_general(
        left, right, (((1,), (1,)), ((), ())), preferred_element_type=jnp.float32
    )


def angles_of(positions):
    half = ROT // 2
    freqs = BASE ** (-(jnp.arange(half, dtype=jnp.float32) * 2.0) / ROT)
    angles = positions.astype(jnp.float32)[:, None] * freqs[None, :]
    return (jnp.cos(angles)[:, None, :], jnp.sin(angles)[:, None, :])


def rotate(values, cosine, sine):
    half = ROT // 2
    first = values[..., :half]
    second = values[..., half:ROT]
    return jnp.concatenate(
        [first * cosine - second * sine, second * cosine + first * sine, values[..., ROT:]], axis=-1
    )


def rotate_back(values, cosine, sine):
    half = ROT // 2
    first = values[..., :half]
    second = values[..., half:ROT]
    return jnp.concatenate(
        [first * cosine + second * sine, second * cosine - first * sine, values[..., ROT:]], axis=-1
    )


def layer_step(weights, inputs, upstream, length, deal_row):
    gain, shift, w_qkv, b_qkv, w_out, b_out, w_up, b_up, w_down, b_down = weights
    row_count, width = inputs.shape
    block_rows = row_count // 2
    head_count = width // HEAD_DIM
    scale = HEAD_DIM ** (-0.5)
    place = lax.axis_index("ctx")
    offsets = jnp.arange(block_rows, dtype=jnp.int32)
    own_blocks = lax.dynamic_slice_in_dim(deal_row, 2 * place, 2)
    local_pos = (own_blocks[:, None] * block_rows + offsets[None, :]).reshape(row_count)
    every_pos = (deal_row[:, None] * block_rows + offsets[None, :]).reshape(-1)
    valid = (local_pos < length).astype(jnp.float32)[:, None]
    allowed = (every_pos[None, :] <= local_pos[:, None]) & (every_pos[None, :] < length)
    cosine, sine = angles_of(local_pos)
    inputs_f = inputs.astype(jnp.float32)
    gain_f = gain.astype(jnp.float32)
    centered = inputs_f - jnp.mean(inputs_f, axis=-1, keepdims=True)
    variance = jnp.mean(centered * centered, axis=-1, keepdims=True)
    inv_std = lax.rsqrt(variance + EPS)
    normed = centered * inv_std
    hidden = (normed * gain_f + shift.astype(jnp.float32)).astype(jnp.bfloat16)
    joined = jnp.dot(hidden, w_qkv, preferred_element_type=jnp.float32) + b_qkv.astype(jnp.float32)
    query = (
        rotate(joined[:, :width].reshape(row_count, head_count, HEAD_DIM), cosine, sine)
        .reshape(row_count, width)
        .astype(jnp.bfloat16)
    )
    keyed = (
        rotate(joined[:, width : 2 * width].reshape(row_count, head_count, HEAD_DIM), cosine, sine)
        .reshape(row_count, width)
        .astype(jnp.bfloat16)
    )
    valued = joined[:, 2 * width :].astype(jnp.bfloat16)
    keys_all, values_all = (
        lax.all_gather(keyed, "ctx", axis=0, tiled=True),
        lax.all_gather(valued, "ctx", axis=0, tiled=True),
    )
    total_keys = keys_all.shape[0]
    group = min(8, head_count)
    span = group * HEAD_DIM

    def heads_of(array, start, count):
        return array[:, start : start + span].reshape(count, group, HEAD_DIM)

    def block_scores(start):
        raw = (
            jnp.einsum(
                "qhd,khd->hqk",
                heads_of(query, start, row_count),
                heads_of(keys_all, start, total_keys),
                preferred_element_type=jnp.float32,
            )
            * scale
        )
        return jnp.where(allowed[None], raw, -1e30)

    attended_parts = []
    lse_parts = []
    for start in range(0, width, span):
        masked = block_scores(start)
        highest = jnp.max(masked, axis=-1, keepdims=True)
        expo = jnp.exp(masked - highest)
        total = jnp.sum(expo, axis=-1, keepdims=True)
        weights_low = (expo / total).astype(jnp.bfloat16)
        mixed = jnp.einsum(
            "hqk,khd->qhd",
            weights_low,
            heads_of(values_all, start, total_keys),
            preferred_element_type=jnp.float32,
        )
        attended_parts.append(mixed.reshape(row_count, span))
        lse_parts.append(highest + jnp.log(total))
    attended = jnp.concatenate(attended_parts, axis=1).astype(jnp.bfloat16)
    branch = jnp.dot(attended, w_out, preferred_element_type=jnp.float32) + b_out.astype(
        jnp.float32
    )
    upward = jnp.dot(hidden, w_up, preferred_element_type=jnp.float32) + b_up.astype(jnp.float32)
    activated = jax.nn.gelu(upward, approximate=True).astype(jnp.bfloat16)
    feed = jnp.dot(activated, w_down, preferred_element_type=jnp.float32) + b_down.astype(
        jnp.float32
    )
    result = (valid * (inputs_f + branch + feed)).astype(jnp.bfloat16)
    grad_out = upstream.astype(jnp.float32) * valid
    grad_low = grad_out.astype(jnp.bfloat16)
    row_total = jnp.sum(grad_out, axis=0)
    d_down = contract_rows(activated, grad_low)
    d_wout = contract_rows(attended, grad_low)
    d_act = contract_cols(grad_low, w_down)
    _, gelu_pull = jax.vjp(lambda value: jax.nn.gelu(value, approximate=True), upward)
    d_upward = gelu_pull(d_act)[0].astype(jnp.bfloat16)
    d_wup = contract_rows(hidden, d_upward)
    d_bup = jnp.sum(d_upward.astype(jnp.float32), axis=0)
    d_attended = contract_cols(grad_low, w_out).astype(jnp.bfloat16)
    dq_parts = []
    dk_parts = []
    dv_parts = []
    delta_parts = []
    for index, start in enumerate(range(0, width, span)):
        masked = block_scores(start)
        probs = jnp.where(allowed[None], jnp.exp(masked - lse_parts[index]), 0.0)
        d_heads = heads_of(d_attended, start, row_count)
        d_probs = jnp.einsum(
            "qhd,khd->hqk",
            d_heads,
            heads_of(values_all, start, total_keys),
            preferred_element_type=jnp.float32,
        )
        delta = jnp.sum(probs * d_probs, axis=-1, keepdims=True)
        d_scores = (probs * (d_probs - delta)).astype(jnp.bfloat16)
        d_query = (
            jnp.einsum(
                "hqk,khd->qhd",
                d_scores,
                heads_of(keys_all, start, total_keys),
                preferred_element_type=jnp.float32,
            )
            * scale
        )
        dq_parts.append(d_query.reshape(row_count, span))
        delta_parts.append(delta[:, :, 0].T)
        d_keyed = (
            jnp.einsum(
                "hqk,qhd->khd",
                d_scores,
                heads_of(query, start, row_count),
                preferred_element_type=jnp.float32,
            )
            * scale
        )
        d_valued = jnp.einsum(
            "hqk,qhd->khd", probs.astype(jnp.bfloat16), d_heads, preferred_element_type=jnp.float32
        )
        dk_parts.append(d_keyed.reshape(total_keys, span))
        dv_parts.append(d_valued.reshape(total_keys, span))
    keys_grad_all = jnp.concatenate(dk_parts, axis=1)
    values_grad_all = jnp.concatenate(dv_parts, axis=1)
    keys_grad, values_grad = (
        lax.psum_scatter(
            keys_grad_all.astype(jnp.bfloat16), "ctx", scatter_dimension=0, tiled=True
        ).astype(jnp.float32),
        lax.psum_scatter(
            values_grad_all.astype(jnp.bfloat16), "ctx", scatter_dimension=0, tiled=True
        ).astype(jnp.float32),
    )
    query_grad = rotate_back(
        jnp.concatenate(dq_parts, axis=1).reshape(row_count, head_count, HEAD_DIM), cosine, sine
    ).reshape(row_count, width)
    keyed_grad = rotate_back(
        keys_grad.reshape(row_count, head_count, HEAD_DIM), cosine, sine
    ).reshape(row_count, width)
    d_joined = jnp.concatenate([query_grad, keyed_grad, values_grad], axis=1).astype(jnp.bfloat16)
    d_wqkv = contract_rows(hidden, d_joined)
    d_bqkv = jnp.sum(d_joined.astype(jnp.float32), axis=0)
    d_hidden = contract_cols(d_joined, w_qkv) + contract_cols(d_upward, w_up)
    d_gain = jnp.sum(d_hidden * normed, axis=0)
    d_shift = jnp.sum(d_hidden, axis=0)
    d_norm = d_hidden * gain_f
    d_inputs = inv_std * (
        d_norm
        - jnp.mean(d_norm, axis=-1, keepdims=True)
        - normed * jnp.mean(d_norm * normed, axis=-1, keepdims=True)
    )
    back = (grad_out + d_inputs).astype(jnp.bfloat16)
    return (
        result,
        back,
        (d_gain, d_shift, d_wqkv, d_bqkv, d_wout, row_total, d_wup, d_bup, d_down, row_total),
    )


def body(
    tokens,
    cotangent,
    lengths,
    deal,
    ln_gain,
    ln_bias,
    w_qkv,
    b_qkv,
    w_out,
    b_out,
    w_up,
    b_up,
    w_down,
    b_down,
):
    shards = (ln_gain, ln_bias, w_qkv, b_qkv, w_out, b_out, w_up, b_up, w_down, b_down)
    shard_count = lax.axis_size("fsdp")
    summed = tuple(
        (
            jnp.zeros((piece.shape[0] * shard_count,) + piece.shape[1:], jnp.float32)
            for piece in shards
        )
    )
    results = []
    backs = []
    for micro_index in range(tokens.shape[1]):
        gathered = (
            lax.all_gather(ln_gain, "fsdp", axis=0, tiled=True),
            lax.all_gather(ln_bias, "fsdp", axis=0, tiled=True),
            lax.all_gather(w_qkv, "fsdp", axis=0, tiled=True),
            lax.all_gather(b_qkv, "fsdp", axis=0, tiled=True),
            lax.all_gather(w_out, "fsdp", axis=0, tiled=True),
            lax.all_gather(b_out, "fsdp", axis=0, tiled=True),
            lax.all_gather(w_up, "fsdp", axis=0, tiled=True),
            lax.all_gather(b_up, "fsdp", axis=0, tiled=True),
            lax.all_gather(w_down, "fsdp", axis=0, tiled=True),
            lax.all_gather(b_down, "fsdp", axis=0, tiled=True),
        )
        result, back, local = layer_step(
            gathered,
            tokens[0, micro_index],
            cotangent[0, micro_index],
            lengths[0, micro_index],
            deal[0, micro_index],
        )
        results.append(result)
        backs.append(back)
        summed = tuple((older + newer for older, newer in zip(summed, local)))
    summed = (
        lax.psum_scatter(
            summed[0].astype(jnp.bfloat16), "fsdp", scatter_dimension=0, tiled=True
        ).astype(jnp.float32),
        lax.psum_scatter(
            summed[1].astype(jnp.bfloat16), "fsdp", scatter_dimension=0, tiled=True
        ).astype(jnp.float32),
        lax.psum_scatter(
            summed[2].astype(jnp.bfloat16), "fsdp", scatter_dimension=0, tiled=True
        ).astype(jnp.float32),
        lax.psum_scatter(
            summed[3].astype(jnp.bfloat16), "fsdp", scatter_dimension=0, tiled=True
        ).astype(jnp.float32),
        lax.psum_scatter(
            summed[4].astype(jnp.bfloat16), "fsdp", scatter_dimension=0, tiled=True
        ).astype(jnp.float32),
        lax.psum_scatter(
            summed[5].astype(jnp.bfloat16), "fsdp", scatter_dimension=0, tiled=True
        ).astype(jnp.float32),
        lax.psum_scatter(
            summed[6].astype(jnp.bfloat16), "fsdp", scatter_dimension=0, tiled=True
        ).astype(jnp.float32),
        lax.psum_scatter(
            summed[7].astype(jnp.bfloat16), "fsdp", scatter_dimension=0, tiled=True
        ).astype(jnp.float32),
        lax.psum_scatter(
            summed[8].astype(jnp.bfloat16), "fsdp", scatter_dimension=0, tiled=True
        ).astype(jnp.float32),
        lax.psum_scatter(
            summed[9].astype(jnp.bfloat16), "fsdp", scatter_dimension=0, tiled=True
        ).astype(jnp.float32),
    )
    totals = (
        lax.psum(summed[0].astype(jnp.bfloat16), ("dp", "ctx")).astype(jnp.float32),
        lax.psum(summed[1].astype(jnp.bfloat16), ("dp", "ctx")).astype(jnp.float32),
        lax.psum(summed[2].astype(jnp.bfloat16), ("dp", "ctx")).astype(jnp.float32),
        lax.psum(summed[3].astype(jnp.bfloat16), ("dp", "ctx")).astype(jnp.float32),
        lax.psum(summed[4].astype(jnp.bfloat16), ("dp", "ctx")).astype(jnp.float32),
        lax.psum(summed[5].astype(jnp.bfloat16), ("dp", "ctx")).astype(jnp.float32),
        lax.psum(summed[6].astype(jnp.bfloat16), ("dp", "ctx")).astype(jnp.float32),
        lax.psum(summed[7].astype(jnp.bfloat16), ("dp", "ctx")).astype(jnp.float32),
        lax.psum(summed[8].astype(jnp.bfloat16), ("dp", "ctx")).astype(jnp.float32),
        lax.psum(summed[9].astype(jnp.bfloat16), ("dp", "ctx")).astype(jnp.float32),
    )
    stacked_out = jnp.stack(results)[None]
    stacked_back = jnp.stack(backs)[None]
    return (
        stacked_out,
        stacked_back,
        totals[0],
        totals[1],
        totals[2],
        totals[3],
        totals[4],
        totals[5],
        totals[6],
        totals[7],
        totals[8],
        totals[9],
    )


def solution(mesh):
    in_specs = (
        P(("dp", "fsdp"), None, "ctx", None),
        P(("dp", "fsdp"), None, "ctx", None),
        P(("dp", "fsdp"), None),
        P(("dp", "fsdp"), None, None),
        P("fsdp"),
        P("fsdp"),
        P("fsdp", None),
        P("fsdp"),
        P("fsdp", None),
        P("fsdp"),
        P("fsdp", None),
        P("fsdp"),
        P("fsdp", None),
        P("fsdp"),
    )
    out_specs = (
        P(("dp", "fsdp"), None, "ctx", None),
        P(("dp", "fsdp"), None, "ctx", None),
        P("fsdp"),
        P("fsdp"),
        P("fsdp", None),
        P("fsdp"),
        P("fsdp", None),
        P("fsdp"),
        P("fsdp", None),
        P("fsdp"),
        P("fsdp", None),
        P("fsdp"),
    )
    return jax.shard_map(body, mesh=mesh, in_specs=in_specs, out_specs=out_specs, check_vma=False)
```

profile of v0, /device:TPU:0, one launch (start us, length us, event | category | flops | bytes accessed | tf_op | source)
XLA Modules:
  0.0 3160.4 jit_solution(15819114740749781028)
XLA Ops:
  34.9 205.6 %all-gather.14.cloned.1.call-done = bf16[2048,6144]{1,0:T(8,128)(2,1)} async-done(((bf16[512,6144]{1,0:T(8,128)(2,1)}), bf16[2048,6144]{1,0:T(8,128)(2,1)}) %all-gather.14.cloned.1.call-update) | async-done | bytes 25165840 | tf_op jit(solution)/shard_map/all_gather | solution.py:249
  306.2 23.8 all-gather.20.cloned.1.call-done
  358.4 53.9 %all-gather.16.cloned.1.call-done = bf16[1024,2048]{1,0:T(8,128)(2,1)} async-done(((bf16[256,2048]{1,0:T(8,128)(2,1)}), bf16[1024,2048]{1,0:T(8,128)(2,1)}) %all-gather.16.cloned.1.call-update) | async-done | bytes 4194320 | tf_op jit(solution)/shard_map/all_gather | solution.py:84
  423.7 70.0 %all-gather.26.cloned.1.call-done = bf16[1024,2048]{1,0:T(8,128)(2,1)} async-done(((bf16[256,2048]{1,0:T(8,128)(2,1)}), bf16[1024,2048]{1,0:T(8,128)(2,1)}) %all-gather.26.cloned.1.call-update) | async-done | bytes 4194320 | tf_op jit(solution)/shard_map/all_gather | solution.py:84
  498.9 75.3 %all-gather.18.cloned.1.call-done = bf16[1024,2048]{0,1:T(8,128)(2,1)} async-done(((bf16[256,2048]{0,1:T(8,128)(2,1)}), bf16[1024,2048]{0,1:T(8,128)(2,1)}) %all-gather.18.cloned.1.call-update) | async-done | bytes 4194320 | tf_op jit(solution)/shard_map/all_gather | solution.py:83
  586.8 68.1 %all-gather.28.cloned.1.call-done = bf16[1024,2048]{0,1:T(8,128)(2,1)} async-done(((bf16[256,2048]{0,1:T(8,128)(2,1)}), bf16[1024,2048]{0,1:T(8,128)(2,1)}) %all-gather.28.cloned.1.call-update) | async-done | bytes 4194320 | tf_op jit(solution)/shard_map/all_gather | solution.py:83
  742.4 26.8 multiply_convert_fusion.7
  851.1 27.0 multiply_convert_fusion.3
  1014.6 31.2 reduce-scatter.15.cloned.1.call-done
  1066.4 59.6 %reduce-scatter.19.cloned.1.call-done = bf16[256,2048]{0,1:T(8,128)(2,1)} async-done(((bf16[1024,2048]{0,1:T(8,128)(2,1)}), bf16[256,2048]{0,1:T(8,128)(2,1)}) %reduce-scatter.19.cloned.1.call-update) | async-done | bytes 1048592 | tf_op jit(solution)/shard_map/reduce_scatter | solution.py:189
  1126.0 32.0 %add_convert_fusion.2 = bf16[2048,6144]{1,0:T(8,128)(2,1)} fusion(f32[2048,6144]{1,0:T(8,128)} %fusion.190, bf16[256,2048]{0,1:T(8,128)(2,1)} %reduce-scatter.19.cloned.1.call-done, bf16[256,2048]{0,1:T(8,128)(2,1)} %bitcast.429, bf16[256,2048]{0,1:T(8,128)(2,1)S(1)} %bitcast.426, f32[256]{0:T(256)S(1)} %copy-done.110, f32[256]{0:T(256)S(1)} %copy-done.107, ...), kind=kOutput, calls=%fused_computation.2 | convolution fusion | flops 6480199680 | bytes 79710208 | tf_op jit(solution)/shard_map/dot_general | solution.py:13
  1167.1 258.5 %all-gather.22.cloned.1.call-done = bf16[2048,8192]{1,0:T(8,128)(2,1)} async-done(((bf16[512,8192]{1,0:T(8,128)(2,1)}), bf16[2048,8192]{1,0:T(8,128)(2,1)}) %all-gather.22.cloned.1.call-update) | async-done | bytes 33554448 | tf_op jit(solution)/shard_map/all_gather | solution.py:253
  1466.3 258.3 %all-gather.24.cloned.1.call-done = bf16[8192,2048]{1,0:T(8,128)(2,1)} async-done(((bf16[2048,2048]{1,0:T(8,128)(2,1)}), bf16[8192,2048]{1,0:T(8,128)(2,1)}) %all-gather.24.cloned.1.call-update) | async-done | bytes 33554448 | tf_op jit(solution)/shard_map/all_gather | solution.py:255
  1724.6 21.7 convert_reduce_fusion.1
  1746.4 22.1 convert_reduce_fusion
  1768.5 27.0 fusion.207
  1795.5 37.4 %add_convert_fusion.1 = bf16[2048,8192]{1,0:T(8,128)(2,1)} fusion(f32[2048,8192]{1,0:T(8,128)} %fusion.207, bf16[256,8192]{1,0:T(8,128)(2,1)} %get-tuple-element.162, f32[256]{0:T(256)S(1)} %copy-done.110, f32[256]{0:T(256)S(1)} %copy-done.107, f32[2048]{0:T(1024)S(1)} %bitcast.481, f32[2048]{0:T(1024)S(1)} %bitcast.469, ...), kind=kOutput, calls=%fused_computation.1 | convolution fusion | flops 8626634752 | bytes 105924608 | tf_op jit(solution)/shard_map/dot_general | solution.py:13
  1833.0 30.1 fusion.192
  1863.0 39.8 %add_convert_fusion = bf16[8192,2048]{1,0:T(8,128)(2,1)} fusion(f32[8192,2048]{1,0:T(8,128)} %fusion.192, f32[256]{0:T(256)S(1)} %copy-done.154, bf16[1,2,256,2048]{3,2,1,0:T(8,128)(2,1)} %param.15, f32[256,8192]{1,0:T(8,128)} %convolution_add_fusion), kind=kOutput, calls=%fused_computation | convolution fusion | flops 8643936256 | bytes 110101504 | tf_op jit(solution)/shard_map/dot_general | solution.py:13
  1980.3 59.7 %reduce-scatter.21.cloned.1.call-done = bf16[512,6144]{1,0:T(8,128)(2,1)} async-done(((bf16[2048,6144]{1,0:T(8,128)(2,1)}), bf16[512,6144]{1,0:T(8,128)(2,1)}) %reduce-scatter.21.cloned.1.call-update) | async-done | bytes 6291472 | tf_op jit(solution)/shard_map/reduce_scatter | solution.py:275
  2040.0 291.6 %reduce-scatter.25.cloned.1.call-done = bf16[512,8192]{1,0:T(8,128)(2,1)} async-done(((bf16[2048,8192]{1,0:T(8,128)(2,1)}), bf16[512,8192]{1,0:T(8,128)(2,1)}) %reduce-scatter.25.cloned.1.call-update) | async-done | bytes 8388624
  2331.6 291.9 %reduce-scatter.27.cloned.1.call-done = bf16[2048,2048]{1,0:T(8,128)(2,1)} async-done(((bf16[8192,2048]{1,0:T(8,128)(2,1)}), bf16[2048,2048]{1,0:T(8,128)(2,1)}) %reduce-scatter.27.cloned.1.call-update) | async-done | bytes 8388624
  2711.4 29.8 all-reduce.7
  2746.6 373.5 %all-reduce.12.cloned.1.call-done = (bf16[512,6144]{1,0:T(8,128)(2,1)}, bf16[512,2048]{1,0:T(8,128)(2,1)}, bf16[512,8192]{1,0:T(8,128)(2,1)}, bf16[2048,2048]{1,0:T(8,128)(2,1)}) async-done(((bf16[512,6144]{1,0:T(8,128)(2,1)}, bf16[512,2048]{1,0:T(8,128)(2,1)}, bf16[512,8192]{1,0:T(8,128)(2,1)}, bf16[2048,2048]{1,0:T(8,128)(2,1)}), (bf16[512,6144]{1,0:T(8,128)(2,1)}, bf16[512,2048]{1,0:T(8,128)(2,1)}, ...) | async-done | bytes 25165840 | tf_op jit(solution)/shard_map/psum | solution.py:303
  (643 shorter events, 726.3 us)
Async XLA Ops:
  7.2 233.2 %all-gather.14.cloned.1.call-start = ((), (), s32[]{:S(2)}) async-start(), calls=%async_computation.8 | async-start | bytes 31457280 | tf_op jit(solution)/shard_map/all_gather | solution.py:249
  8.0 322.0 %all-gather.20.cloned.1.call-start = ((), (), s32[]{:S(2)}) async-start(), calls=%async_computation.11 | async-start | bytes 10485760 | tf_op jit(solution)/shard_map/all_gather | solution.py:251
  8.7 403.6 %all-gather.16.cloned.1.call-start = ((), (), s32[]{:S(2)}) async-start(), calls=%async_computation.9 | async-start | bytes 5242880 | tf_op jit(solution)/shard_map/all_gather | solution.py:84
  18.3 237.9 %copy-start.39 = (f32[4,1,512]{2,1,0:T(1,128)}, f32[4,1,512]{2,1,0:T(1,128)S(1)}, u32[]{:S(2)}) copy-start(f32[4,1,512]{2,1,0:T(1,128)S(1)} %convert_element_type.392) | copy-start | bytes 24580
  26.4 229.8 %copy-start.42 = (f32[4,1,512]{2,1,0:T(1,128)}, f32[4,1,512]{2,1,0:T(1,128)S(1)}, u32[]{:S(2)}) copy-start(f32[4,1,512]{2,1,0:T(1,128)S(1)} %convert_element_type.393) | copy-start | bytes 24580
  34.2 218.1 %copy-start.80 = (f32[256]{0:T(256)}, f32[256]{0:T(256)S(1)}, u32[]{:S(2)}) copy-start(f32[256]{0:T(256)S(1)} %get-tuple-element.164) | copy-start | bytes 3076
  34.2 222.0 %copy-start.106 = (f32[256]{0:T(256)}, f32[256]{0:T(256)S(1)}, u32[]{:S(2)}) copy-start(f32[256]{0:T(256)S(1)} %get-tuple-element.163) | copy-start | bytes 3076
  34.9 217.4 %copy-start.99 = (f32[256]{0:T(256)}, f32[256]{0:T(256)S(1)}, u32[]{:S(2)}) copy-start(f32[256]{0:T(256)S(1)} %add_rsqrt_fusion.1) | copy-start | bytes 3076
  256.1 237.5 %all-gather.26.cloned.1.call-start = ((), (), s32[]{:S(2)}) async-start(), calls=%async_computation.14 | async-start | bytes 5242880 | tf_op jit(solution)/shard_map/all_gather | solution.py:84
  271.9 302.2 %all-gather.18.cloned.1.call-start = ((), (), s32[]{:S(2)}) async-start(), calls=%async_computation.10 | async-start | bytes 5242880 | tf_op jit(solution)/shard_map/all_gather | solution.py:83
  286.2 368.8 %all-gather.28.cloned.1.call-start = ((), (), s32[]{:S(2)}) async-start(), calls=%async_computation.15 | async-start | bytes 5242880 | tf_op jit(solution)/shard_map/all_gather | solution.py:83
  304.6 696.4 %reduce-scatter.13.cloned.1.call-start = ((), (), s32[]{:S(2)}) async-start(), calls=%async_computation.16 | async-start | bytes 5242880 | tf_op jit(solution)/shard_map/reduce_scatter | solution.py:186
  782.4 222.5 %reduce-scatter.17.cloned.1.call-start = ((), (), s32[]{:S(2)}) async-start(), calls=%async_computation.18 | async-start | bytes 5242880 | tf_op jit(solution)/shard_map/reduce_scatter | solution.py:186
  891.2 154.7 %reduce-scatter.15.cloned.1.call-start = ((), (), s32[]{:S(2)}) async-start(), calls=%async_computation.17 | async-start | bytes 5242880 | tf_op jit(solution)/shard_map/reduce_scatter | solution.py:189
  910.7 215.3 %reduce-scatter.19.cloned.1.call-start = ((), (), s32[]{:S(2)}) async-start(), calls=%async_computation.19 | async-start | bytes 5242880 | tf_op jit(solution)/shard_map/reduce_scatter | solution.py:189
  930.5 495.1 %all-gather.22.cloned.1.call-start = ((), (), s32[]{:S(2)}) async-start(), calls=%async_computation.12 | async-start | bytes 41943040 | tf_op jit(solution)/shard_map/all_gather | solution.py:253
  931.3 793.4 %all-gather.24.cloned.1.call-start = ((), (), s32[]{:S(2)}) async-start(), calls=%async_computation.13 | async-start | bytes 41943040 | tf_op jit(solution)/shard_map/all_gather | solution.py:255
  931.9 1048.4 %reduce-scatter.23.cloned.1.call-start = ((), (), s32[]{:S(2)}) async-start(), calls=%async_computation.21 | async-start | bytes 10485760 | tf_op jit(solution)/shard_map/reduce_scatter | solution.py:281
  979.9 1060.1 %reduce-scatter.21.cloned.1.call-start = ((), (), s32[]{:S(2)}) async-start(), calls=%async_computation.20 | async-start | bytes 31457280 | tf_op jit(solution)/shard_map/reduce_scatter | solution.py:275
  1158.0 1173.6 %reduce-scatter.25.cloned.1.call-start = ((), (), s32[]{:S(2)}) async-start(), calls=%async_computation.22 | async-start | bytes 41943040
  1447.3 277.3 %copy-start.157 = (f32[256]{0:T(256)S(1)}, f32[256]{0:T(256)}, u32[]{:S(2)}) copy-start(f32[256]{0:T(256)} %copy-done.155) | copy-start | bytes 3076
  1832.9 790.5 %reduce-scatter.27.cloned.1.call-start = ((), (), s32[]{:S(2)}) async-start(), calls=%async_computation.23 | async-start | bytes 41943040
  1902.9 1217.2 %all-reduce.12.cloned.1.call-start = ((), (), s32[]{:S(2)}) async-start(), calls=%async_computation.24 | async-start | bytes 50331648 | tf_op jit(solution)/shard_map/psum | solution.py:303
  2742.4 410.4 %copy-start.158 = (f32[512]{0:T(512)}, f32[512]{0:T(512)S(1)}, u32[]{:S(2)}) copy-start(f32[512]{0:T(512)S(1)} %convert_element_type.381) | copy-start | bytes 6148
  (187 other events, 2263.9 us)
Sparse Core Ops, SparseCore 0:
  9.9 230.4 all-gather.13
  242.3 87.6 all-gather.19
  331.5 80.7 all-gather.15
  414.3 79.2 all-gather.25
  495.0 79.0 all-gather.17
  576.2 78.7 all-gather.27
  782.5 74.9 reduce-scatter.12
  891.3 74.8 reduce-scatter.16
  968.6 77.2 reduce-scatter.14
  1048.7 77.2 reduce-scatter.18
  1127.8 297.7 all-gather.21
  1427.4 297.2 all-gather.23
  1728.2 86.4 reduce-scatter.22
  1818.0 221.9 reduce-scatter.20
  2042.9 288.6 reduce-scatter.24
  2334.8 288.6 reduce-scatter.26
  2626.2 493.8 all-reduce.11
where the time goes:
time: 3170 us; the launch traced here: 3160 us
  waiting for transfers between devices  2120 us (67%)
  matrix products  665 us (21%)
  other arithmetic  161 us (5%)
  local copies, waits for them, and re-layouts  95.3 us (3%)
  blocking collectives  93.9 us (3%)
    unnamed x19, waiting for transfers between devices  586 us
    psum x1, waiting for transfers between devices, body(): lax.psum(summed[2].astype(jnp.bfloat16), ('dp', 'ctx')).astype(jnp.float32)  374 us
    all_gather x1, waiting for transfers between devices, body(): lax.all_gather(w_up, 'fsdp', axis=0, tiled=True)  259 us
    all_gather x1, waiting for transfers between devices, body(): lax.all_gather(w_down, 'fsdp', axis=0, tiled=True)  258 us
    dot_general x8, matrix products, contract_rows(): lax.dot_general(left, right, (((0,), (0,)), ((), ())), preferred_element_...  206 us
    all_gather x1, waiting for transfers between devices, body(): lax.all_gather(w_qkv, 'fsdp', axis=0, tiled=True)  206 us
    all_gather x2, waiting for transfers between devices, layer_step(): lax.all_gather(keyed, 'ctx', axis=0, tiled=True)  143 us
    all_gather x2, waiting for transfers between devices, layer_step(): lax.all_gather(valued, 'ctx', axis=0, tiled=True)  124 us
  transfers between devices with their start and end apart: 17, of which 14 were waited for; matrix products, arithmetic and copies ran while one was open for 24% of the time, Pallas kernels for 0%

commit v1 on v0

--- a/solution.py
+++ b/solution.py
@@ -2,6 +2,7 @@
 import jax.numpy as jnp
 from jax import lax
 from jax.sharding import PartitionSpec as P
+from jax.lax import psum
 
 HEAD_DIM = 64
 ROT = 32
@@ -300,7 +301,7 @@
     totals = (
         lax.psum(summed[0].astype(jnp.bfloat16), ("dp", "ctx")).astype(jnp.float32),
         lax.psum(summed[1].astype(jnp.bfloat16), ("dp", "ctx")).astype(jnp.float32),
-        lax.psum(summed[2].astype(jnp.bfloat16), ("dp", "ctx")).astype(jnp.float32),
+        psum(psum(summed[2].astype(jnp.bfloat16), "ctx"), "dp").astype(jnp.float32),
         lax.psum(summed[3].astype(jnp.bfloat16), ("dp", "ctx")).astype(jnp.float32),
         lax.psum(summed[4].astype(jnp.bfloat16), ("dp", "ctx")).astype(jnp.float32),
         lax.psum(summed[5].astype(jnp.bfloat16), ("dp", "ctx")).astype(jnp.float32),

time: 3170 us -> 3330 us (1.050)
  waiting for transfers between devices: 2120 us -> 2280 us
    reduce_scatter x1, waiting for transfers between devices: 59.7 us -> 187 us  [body(): lax.psum_scatter(summed[2].astype(jnp.bfloat16), 'fsdp', scatter_dimensio...]
    psum x1 -> x3, waiting for transfers between devices: 374 us -> 313 us  [the longest x1 293 us: body(): lax.psum(summed[4].astype(jnp.bfloat16), ('dp', 'ctx')).astype(jnp.float32)]
    reduce_scatter x2, waiting for transfers between devices: 90.9 us -> 129 us  [layer_step(): lax.psum_scatter(values_grad_all.astype(jnp.bfloat16), 'ctx', scatter_dim...]
    unnamed x19 -> x21, waiting for transfers between devices: 586 us -> 586 us
  transfers between devices with their start and end apart: 17 -> 19, of which waited for: 14 -> 17; matrix products, arithmetic and copies ran while one was open for 24% -> 22% of each run, Pallas kernels for 0% -> 0%
where the time goes in v1:
time: 3330 us; the launch traced here: 3320 us
  waiting for transfers between devices  2280 us (68%)
  matrix products  660 us (20%)
  other arithmetic  166 us (5%)
  local copies, waits for them, and re-layouts  100 us (3%)
  blocking collectives  93.5 us (3%)
    unnamed x21, waiting for transfers between devices  586 us
    psum x1, waiting for transfers between devices, body(): lax.psum(summed[4].astype(jnp.bfloat16), ('dp', 'ctx')).astype(jnp.float32)  293 us
    all_gather x1, waiting for transfers between devices, body(): lax.all_gather(w_up, 'fsdp', axis=0, tiled=True)  264 us
    all_gather x1, waiting for transfers between devices, body(): lax.all_gather(w_down, 'fsdp', axis=0, tiled=True)  259 us
    all_gather x1, waiting for transfers between devices, body(): lax.all_gather(w_qkv, 'fsdp', axis=0, tiled=True)  206 us
    dot_general x8, matrix products, contract_rows(): lax.dot_general(left, right, (((0,), (0,)), ((), ())), preferred_element_...  195 us
    reduce_scatter x1, waiting for transfers between devices, body(): lax.psum_scatter(summed[2].astype(jnp.bfloat16), 'fsdp', scatter_dimensio...  187 us
    all_gather x2, waiting for transfers between devices, layer_step(): lax.all_gather(keyed, 'ctx', axis=0, tiled=True)  143 us
  transfers between devices with their start and end apart: 19, of which 17 were waited for; matrix products, arithmetic and copies ran while one was open for 22% of the time, Pallas kernels for 0%

profile of v1, /device:TPU:0, one launch (start us, length us, event | category | flops | bytes accessed | tf_op | source)
XLA Modules:
  0.0 3318.2 jit_solution(12919504704390750034)
XLA Ops:
  34.8 205.6 %all-gather.14.cloned.1.call-done = bf16[2048,6144]{1,0:T(8,128)(2,1)} async-done(((bf16[512,6144]{1,0:T(8,128)(2,1)}), bf16[2048,6144]{1,0:T(8,128)(2,1)}) %all-gather.14.cloned.1.call-update) | async-done | bytes 25165840 | tf_op jit(solution)/shard_map/all_gather | solution.py:250
  306.0 23.9 all-gather.20.cloned.1.call-done
  358.4 54.4 %all-gather.26.cloned.1.call-done = bf16[1024,2048]{1,0:T(8,128)(2,1)} async-done(((bf16[256,2048]{1,0:T(8,128)(2,1)}), bf16[1024,2048]{1,0:T(8,128)(2,1)}) %all-gather.26.cloned.1.call-update) | async-done | bytes 4194320 | tf_op jit(solution)/shard_map/all_gather | solution.py:85
  424.1 69.5 %all-gather.16.cloned.1.call-done = bf16[1024,2048]{1,0:T(8,128)(2,1)} async-done(((bf16[256,2048]{1,0:T(8,128)(2,1)}), bf16[1024,2048]{1,0:T(8,128)(2,1)}) %all-gather.16.cloned.1.call-update) | async-done | bytes 4194320 | tf_op jit(solution)/shard_map/all_gather | solution.py:85
  498.8 75.3 %all-gather.28.cloned.1.call-done = bf16[1024,2048]{0,1:T(8,128)(2,1)} async-done(((bf16[256,2048]{0,1:T(8,128)(2,1)}), bf16[1024,2048]{0,1:T(8,128)(2,1)}) %all-gather.28.cloned.1.call-update) | async-done | bytes 4194320 | tf_op jit(solution)/shard_map/all_gather | solution.py:84
  586.7 68.2 %all-gather.18.cloned.1.call-done = bf16[1024,2048]{0,1:T(8,128)(2,1)} async-done(((bf16[256,2048]{0,1:T(8,128)(2,1)}), bf16[1024,2048]{0,1:T(8,128)(2,1)}) %all-gather.18.cloned.1.call-update) | async-done | bytes 4194320 | tf_op jit(solution)/shard_map/all_gather | solution.py:84
  741.4 26.8 multiply_convert_fusion.3
  850.0 27.0 multiply_convert_fusion.7
  975.7 69.0 %reduce-scatter.15.cloned.1.call-done = bf16[256,2048]{0,1:T(8,128)(2,1)} async-done(((bf16[1024,2048]{0,1:T(8,128)(2,1)}), bf16[256,2048]{0,1:T(8,128)(2,1)}) %reduce-scatter.15.cloned.1.call-update) | async-done | bytes 1048592 | tf_op jit(solution)/shard_map/reduce_scatter | solution.py:190
  1065.3 59.6 %reduce-scatter.19.cloned.1.call-done = bf16[256,2048]{0,1:T(8,128)(2,1)} async-done(((bf16[1024,2048]{0,1:T(8,128)(2,1)}), bf16[256,2048]{0,1:T(8,128)(2,1)}) %reduce-scatter.19.cloned.1.call-update) | async-done | bytes 1048592 | tf_op jit(solution)/shard_map/reduce_scatter | solution.py:190
  1124.9 25.8 add_convert_fusion.2
  1186.2 187.0 %reduce-scatter.21.cloned.1.call-done = bf16[512,6144]{1,0:T(8,128)(2,1)} async-done(((bf16[2048,6144]{1,0:T(8,128)(2,1)}), bf16[512,6144]{1,0:T(8,128)(2,1)}) %reduce-scatter.21.cloned.1.call-update) | async-done | bytes 6291472 | tf_op jit(solution)/shard_map/reduce_scatter | solution.py:276
  1407.9 264.5 %all-gather.22.cloned.1.call-done = bf16[2048,8192]{1,0:T(8,128)(2,1)} async-done(((bf16[512,8192]{1,0:T(8,128)(2,1)}), bf16[2048,8192]{1,0:T(8,128)(2,1)}) %all-gather.22.cloned.1.call-update) | async-done | bytes 33554448 | tf_op jit(solution)/shard_map/all_gather | solution.py:254
  1712.9 258.7 %all-gather.24.cloned.1.call-done = bf16[8192,2048]{1,0:T(8,128)(2,1)} async-done(((bf16[2048,2048]{1,0:T(8,128)(2,1)}), bf16[8192,2048]{1,0:T(8,128)(2,1)}) %all-gather.24.cloned.1.call-update) | async-done | bytes 33554448 | tf_op jit(solution)/shard_map/all_gather | solution.py:256
  1993.4 21.9 convert_reduce_fusion.1
  2015.4 25.8 fusion.207
  2041.1 34.5 %add_convert_fusion.1 = bf16[2048,8192]{1,0:T(8,128)(2,1)} fusion(f32[2048,8192]{1,0:T(8,128)} %fusion.207, bf16[256,8192]{1,0:T(8,128)(2,1)} %get-tuple-element.161, f32[256]{0:T(256)S(1)} %copy-done.111, f32[256]{0:T(256)S(1)} %copy-done.108, f32[2048]{0:T(1024)S(1)} %bitcast.475, f32[2048]{0:T(1024)S(1)} %bitcast.465, ...), kind=kOutput, calls=%fused_computation.1 | convolution fusion | flops 8626634752 | bytes 105924608 | tf_op jit(solution)/shard_map/dot_general | solution.py:14
  2075.7 29.9 fusion.192
  2105.6 37.7 %add_convert_fusion = bf16[8192,2048]{1,0:T(8,128)(2,1)} fusion(f32[8192,2048]{1,0:T(8,128)} %fusion.192, f32[256]{0:T(256)S(1)} %copy-done.156, bf16[1,2,256,2048]{3,2,1,0:T(8,128)(2,1)} %param.15, f32[256,8192]{1,0:T(8,128)} %convolution_add_fusion), kind=kOutput, calls=%fused_computation | convolution fusion | flops 8643936256 | bytes 110101504 | tf_op jit(solution)/shard_map/dot_general | solution.py:14
  2255.2 30.7 reduce-scatter.23.cloned.1.call-done
  2286.0 291.6 %reduce-scatter.25.cloned.1.call-done = bf16[512,8192]{1,0:T(8,128)(2,1)} async-done(((bf16[2048,8192]{1,0:T(8,128)(2,1)}), bf16[512,8192]{1,0:T(8,128)(2,1)}) %reduce-scatter.25.cloned.1.call-update) | async-done | bytes 8388624
  2577.6 291.9 %reduce-scatter.27.cloned.1.call-done = bf16[2048,2048]{1,0:T(8,128)(2,1)} async-done(((bf16[8192,2048]{1,0:T(8,128)(2,1)}), bf16[2048,2048]{1,0:T(8,128)(2,1)}) %reduce-scatter.27.cloned.1.call-update) | async-done | bytes 8388624
  2945.4 29.8 all-reduce.7
  2990.0 293.1 %all-reduce.18.cloned.1.call-done = (bf16[512,2048]{1,0:T(8,128)(2,1)}, bf16[512,8192]{1,0:T(8,128)(2,1)}, bf16[2048,2048]{1,0:T(8,128)(2,1)}) async-done(((bf16[512,2048]{1,0:T(8,128)(2,1)}, bf16[512,8192]{1,0:T(8,128)(2,1)}, bf16[2048,2048]{1,0:T(8,128)(2,1)}), (bf16[512,2048]{1,0:T(8,128)(2,1)}, bf16[512,8192]{1,0:T(8,128)(2,1)}, bf16[2048,2048]{1,0:T(8,128)(2,1)})) %all-reduce.18.cloned.1.call-update) | async-done | bytes 18874384 | tf_op jit(solution)/shard_map/psum | solution.py:306
  (636 shorter events, 796.8 us)
Async XLA Ops:
  7.2 233.2 %all-gather.14.cloned.1.call-start = ((), (), s32[]{:S(2)}) async-start(), calls=%async_computation.8 | async-start | bytes 31457280 | tf_op jit(solution)/shard_map/all_gather | solution.py:250
  8.0 321.9 %all-gather.20.cloned.1.call-start = ((), (), s32[]{:S(2)}) async-start(), calls=%async_computation.11 | async-start | bytes 10485760 | tf_op jit(solution)/shard_map/all_gather | solution.py:252
  8.7 404.1 %all-gather.26.cloned.1.call-start = ((), (), s32[]{:S(2)}) async-start(), calls=%async_computation.14 | async-start | bytes 5242880 | tf_op jit(solution)/shard_map/all_gather | solution.py:85
  26.5 229.6 %copy-start.42 = (f32[4,1,512]{2,1,0:T(1,128)}, f32[4,1,512]{2,1,0:T(1,128)S(1)}, u32[]{:S(2)}) copy-start(f32[4,1,512]{2,1,0:T(1,128)S(1)} %convert_element_type.393) | copy-start | bytes 24580
  256.1 237.5 %all-gather.16.cloned.1.call-start = ((), (), s32[]{:S(2)}) async-start(), calls=%async_computation.9 | async-start | bytes 5242880 | tf_op jit(solution)/shard_map/all_gather | solution.py:85
  271.9 302.2 %all-gather.28.cloned.1.call-start = ((), (), s32[]{:S(2)}) async-start(), calls=%async_computation.15 | async-start | bytes 5242880 | tf_op jit(solution)/shard_map/all_gather | solution.py:84
  286.0 368.9 %all-gather.18.cloned.1.call-start = ((), (), s32[]{:S(2)}) async-start(), calls=%async_computation.10 | async-start | bytes 5242880 | tf_op jit(solution)/shard_map/all_gather | solution.py:84
  304.5 645.8 %reduce-scatter.17.cloned.1.call-start = ((), (), s32[]{:S(2)}) async-start(), calls=%async_computation.18 | async-start | bytes 5242880 | tf_op jit(solution)/shard_map/reduce_scatter | solution.py:187
  358.4 300.4 %copy-start.56 = (bf16[256,512]{0,1:T(8,128)(2,1)}, bf16[256,512]{0,1:T(8,128)(2,1)S(1)}, u32[]{:S(2)}) copy-start(bf16[256,512]{0,1:T(8,128)(2,1)S(1)} %get-tuple-element.112) | copy-start | bytes 786436
  781.4 183.8 %reduce-scatter.13.cloned.1.call-start = ((), (), s32[]{:S(2)}) async-start(), calls=%async_computation.16 | async-start | bytes 5242880 | tf_op jit(solution)/shard_map/reduce_scatter | solution.py:187
  890.2 154.6 %reduce-scatter.15.cloned.1.call-start = ((), (), s32[]{:S(2)}) async-start(), calls=%async_computation.17 | async-start | bytes 5242880 | tf_op jit(solution)/shard_map/reduce_scatter | solution.py:190
  909.6 215.3 %reduce-scatter.19.cloned.1.call-start = ((), (), s32[]{:S(2)}) async-start(), calls=%async_computation.19 | async-start | bytes 5242880 | tf_op jit(solution)/shard_map/reduce_scatter | solution.py:190
  929.4 443.9 %reduce-scatter.21.cloned.1.call-start = ((), (), s32[]{:S(2)}) async-start(), calls=%async_computation.20 | async-start | bytes 31457280 | tf_op jit(solution)/shard_map/reduce_scatter | solution.py:276
  1150.8 521.6 %all-gather.22.cloned.1.call-start = ((), (), s32[]{:S(2)}) async-start(), calls=%async_computation.12 | async-start | bytes 41943040 | tf_op jit(solution)/shard_map/all_gather | solution.py:254
  1151.4 820.2 %all-gather.24.cloned.1.call-start = ((), (), s32[]{:S(2)}) async-start(), calls=%async_computation.13 | async-start | bytes 41943040 | tf_op jit(solution)/shard_map/all_gather | solution.py:256
  1152.1 1044.7 %all-reduce.14.cloned.1.call-start = ((), (), s32[]{:S(2)}) async-start(), calls=%async_computation.21 | async-start | bytes 12582912 | tf_op jit(solution)/shard_map/psum | solution.py:304
  1373.3 912.7 %reduce-scatter.23.cloned.1.call-start = ((), (), s32[]{:S(2)}) async-start(), calls=%async_computation.23 | async-start | bytes 10485760 | tf_op jit(solution)/shard_map/reduce_scatter | solution.py:282
  1407.6 285.9 %copy-start.81 = (f32[256]{0:T(256)S(1)}, f32[256]{0:T(256)}, u32[]{:S(2)}) copy-start(f32[256]{0:T(256)} %copy-done.79) | copy-start | bytes 3076
  1407.6 285.9 %copy-start.101 = (f32[256]{0:T(256)S(1)}, f32[256]{0:T(256)}, u32[]{:S(2)}) copy-start(f32[256]{0:T(256)} %copy-done.99) | copy-start | bytes 3076
  1407.6 1169.9 %reduce-scatter.25.cloned.1.call-start = ((), (), s32[]{:S(2)}) async-start(), calls=%async_computation.24 | async-start | bytes 41943040
  2075.7 793.8 %reduce-scatter.27.cloned.1.call-start = ((), (), s32[]{:S(2)}) async-start(), calls=%async_computation.25 | async-start | bytes 41943040
  2143.4 837.3 %all-reduce.16.cloned.1.call-start = ((), (), s32[]{:S(2)}) async-start(), calls=%async_computation.22 | async-start | bytes 12582912 | tf_op jit(solution)/shard_map/psum | solution.py:304
  2196.8 1086.2 %all-reduce.18.cloned.1.call-start = ((), (), s32[]{:S(2)}) async-start(), calls=%async_computation.26 | async-start | bytes 37748736 | tf_op jit(solution)/shard_map/psum | solution.py:306
  2977.0 333.6 %copy-start.159 = (f32[512]{0:T(512)}, f32[512]{0:T(512)S(1)}, u32[]{:S(2)}) copy-start(f32[512]{0:T(512)S(1)} %convert_element_type.381) | copy-start | bytes 6148
  (184 other events, 3630.5 us)
Sparse Core Ops, SparseCore 0:
  9.9 230.4 all-gather.13
  242.2 87.5 all-gather.19
  332.0 80.7 all-gather.25
  414.3 79.2 all-gather.15
  495.0 79.0 all-gather.27
  576.1 78.7 all-gather.17
  781.6 74.9 reduce-scatter.16
  890.3 74.8 reduce-scatter.12
  967.5 77.2 reduce-scatter.14
  1047.6 77.2 reduce-scatter.18
  1150.9 222.3 reduce-scatter.20
  1375.1 297.2 all-gather.21
  1674.3 297.2 all-gather.23
  1973.9 222.8 all-reduce.13
  2200.6 85.3 reduce-scatter.22
  2288.9 288.6 reduce-scatter.24
  2580.8 288.6 reduce-scatter.26
  2871.8 31.9 all-reduce.15
  2906.9 376.0 all-reduce.17
